TPU v7x, 128 devices: a whole 4x4x4 slice. The times are simulated.
128 devices in a mesh: row: 16 (over y, x), col: 8 (over z, core).
Axes of the slice: x: 4, y: 4, z: 4, core: 2. Of those that a mesh axis runs over, the one named last changes fastest.
Arguments:
- tokens: bfloat16 [16384, 1280], P(('row', 'col')), may hold values from -6 to 6
- image_sizes: int32 [16, 8], replicated, may hold values from 1 to 48, 256 in all within a row
- slot_of: int32 [128], replicated, may hold values from 0 to 127, as said below
- ln_gain: float32 [1, 2, 1280], replicated, may hold values from 0.25 to 1.75
- ln_bias: float32 [1, 2, 1280], replicated, may hold values from -3 to 3
- w_qkv: bfloat16 [1, 1280, 3840], P(None, 'row', 'col')
- w_out: bfloat16 [1, 1280, 1280], P(None, 'col', 'row'), may hold values from -0.15625 to 0.15625
- w_up: bfloat16 [1, 1280, 5120], P(None, 'row', 'col'), may hold values from -0.15625 to 0.15625
- w_down: bfloat16 [1, 5120, 1280], P(None, 'col', 'row'), may hold values from -0.078125 to 0.078125
- merge_gain: float32 [1280], replicated, may hold values from 0.25 to 1.75
- merge_bias: float32 [1280], replicated, may hold values from -3 to 3
- w_merge: bfloat16 [5120, 4096], P('row', 'col'), may hold values from -0.078125 to 0.078125
Outputs:
- merged_out: bfloat16 [6144, 4096], P('row', 'col')
- req_norm: float32 [128], P('row')
- req_max: float32 [128], P('row')
Inputs may be any that keep to these rules, and one draw needn't show every extreme that they name: Each row of image_sizes sums to 256 and holds 48 at least once. A permutation of the slots. Request g * 8 + j goes to the row group slot_of // 8, which holds 8 slots. No row group sends more than one request to any row group.
All inputs are finite; a program needn't handle non-finite values.
Results may differ from a plain program's by a relative error of at most 0.018.
The roundings to bfloat16 on the way count: a program that leaves them out, or rounds other values in their place, can miss the bound.
Values may be sent and summed in bfloat16 or wider, within the bound.
A program may use at most 64 MiB of HBM per device.

v0:
```python
import jax
import jax.numpy as jnp
from jax import lax
from jax.sharding import PartitionSpec as P

D = 1280
HEAD_DIM = 80
OUT = 4096
IMG_ROW = 8


def layer_norm(values, gain, bias):
    center = jnp.mean(values, axis=-1, keepdims=True)
    shifted = values - center
    spread = jnp.mean(shifted * shifted, axis=-1, keepdims=True)
    return shifted * lax.rsqrt(spread + 1e-06) * gain + bias


def segment_ids(sizes_row, count):
    bounds = jnp.cumsum(sizes_row)
    merged_index = jnp.arange(count, dtype=jnp.int32) // 4
    return jnp.sum((merged_index[:, None] >= bounds[None, :]).astype(jnp.int32), axis=1)


def attend(qkv, segments):
    count = qkv.shape[0]
    width = min(512, count)
    query = qkv[:, :, 0]
    keys = qkv[:, :, 1]
    values = qkv[:, :, 2]
    results = []
    for offset in range(0, count, width):
        scores = jnp.einsum(
            "qhd,khd->hqk", query[offset : offset + width], keys, preferred_element_type=jnp.float32
        ) * HEAD_DIM ** (-0.5)
        same = segments[offset : offset + width, None] == segments[None, :]
        scores = jnp.where(same[None], scores, -1e30)
        peak = jnp.max(scores, axis=-1, keepdims=True)
        expo = jnp.exp(scores - peak)
        weights = (expo / jnp.sum(expo, axis=-1, keepdims=True)).astype(jnp.bfloat16)
        context = jnp.einsum("hqk,khd->qhd", weights, values, preferred_element_type=jnp.float32)
        results.append(context.astype(jnp.bfloat16).reshape(width, -1))
    return jnp.concatenate(results, axis=0)


def local(
    tokens,
    image_sizes,
    slot_of,
    ln_gain,
    ln_bias,
    w_qkv,
    w_out,
    w_up,
    w_down,
    merge_gain,
    merge_bias,
    w_merge,
):
    n_col = lax.axis_size("col")
    row_index = lax.axis_index("row")
    tok_dev = tokens.shape[0]
    tok_row = tok_dev * n_col
    merged_row = tok_row // 4
    most = merged_row * 3 // 16
    sizes_here = lax.dynamic_index_in_dim(image_sizes, row_index, 0, keepdims=False)
    segments = segment_ids(sizes_here, tok_row)
    stream = tokens
    normed = layer_norm(stream.astype(jnp.float32), ln_gain[0, 0], ln_bias[0, 0]).astype(
        jnp.bfloat16
    )
    normed_all = lax.all_gather(normed, "col", axis=0, tiled=True)
    left_part = normed_all
    qkv = jnp.dot(
        left_part,
        lax.all_gather(w_qkv[0], "row", axis=0, tiled=True),
        preferred_element_type=jnp.float32,
    )
    qkv = qkv.astype(jnp.bfloat16).reshape(tok_row, -1, 3, HEAD_DIM)
    context = attend(qkv, segments)
    attn_terms = jnp.dot(
        context,
        lax.all_gather(w_out[0], "row", axis=1, tiled=True),
        preferred_element_type=jnp.float32,
    )
    attn_out = lax.psum_scatter(
        attn_terms.astype(jnp.bfloat16), "col", scatter_dimension=0, tiled=True
    ).astype(jnp.float32)
    stream = (stream.astype(jnp.float32) + attn_out).astype(jnp.bfloat16)
    normed = layer_norm(stream.astype(jnp.float32), ln_gain[0, 1], ln_bias[0, 1]).astype(
        jnp.bfloat16
    )
    normed_mlp = lax.all_gather(normed, "col", axis=0, tiled=True)
    left_part = normed_mlp
    up_value = jnp.dot(
        left_part,
        lax.all_gather(w_up[0], "row", axis=0, tiled=True),
        preferred_element_type=jnp.float32,
    )
    hidden = jax.nn.gelu(up_value, approximate=False).astype(jnp.bfloat16)
    mlp_terms = jnp.dot(
        hidden,
        lax.all_gather(w_down[0], "row", axis=1, tiled=True),
        preferred_element_type=jnp.float32,
    )
    mlp_out = lax.psum_scatter(
        mlp_terms.astype(jnp.bfloat16), "col", scatter_dimension=0, tiled=True
    ).astype(jnp.float32)
    stream = (stream.astype(jnp.float32) + mlp_out).astype(jnp.bfloat16)
    merged = layer_norm(stream.astype(jnp.float32), merge_gain, merge_bias).astype(jnp.bfloat16)
    merged = merged.reshape(tok_dev // 4, 4 * D)
    merged_all = lax.all_gather(merged, "col", axis=0, tiled=True)
    out_dev = w_merge.shape[1]
    left_part = merged_all
    projected = jnp.dot(
        left_part,
        lax.all_gather(w_merge, "row", axis=0, tiled=True),
        preferred_element_type=jnp.float32,
    ).astype(jnp.bfloat16)
    reqs = slot_of.shape[0]
    numbers = jnp.arange(reqs, dtype=jnp.int32)
    req_at_slot = jnp.sum(
        jnp.where(slot_of[None, :] == numbers[:, None], numbers[None, :], 0), axis=1
    )
    starts = jnp.cumsum(image_sizes, axis=1) - image_sizes
    starts_flat = starts.reshape(-1)
    sizes_flat = image_sizes.reshape(-1)
    inner = jnp.arange(most, dtype=jnp.int32)
    request = lax.dynamic_slice_in_dim(req_at_slot, row_index * IMG_ROW, IMG_ROW)
    group = request // IMG_ROW
    source = ((group * merged_row + starts_flat[request])[:, None] + inner[None, :]).reshape(-1)
    valid = (inner[None, :] < sizes_flat[request][:, None]).reshape(-1)
    rows_init = jnp.zeros((IMG_ROW * most, out_dev), jnp.bfloat16)
    piece = lax.all_gather(projected, "row", axis=0, tiled=True)
    inside = valid & (source >= 0) & (source < piece.shape[0])
    taken = jnp.take(piece, jnp.clip(source, 0, piece.shape[0] - 1), axis=0)
    placed = jnp.where(inside[:, None], taken, rows_init)
    blocks = placed.astype(jnp.float32).reshape(IMG_ROW, most, out_dev)
    squares = jnp.sum(blocks * blocks, axis=(1, 2))
    peaks = jnp.max(jnp.abs(blocks), axis=(1, 2))
    squares = lax.psum(squares, "col")
    peaks = lax.pmax(peaks, "col")
    slot_size = sizes_flat[request].astype(jnp.float32)
    req_norm = jnp.sqrt(squares / (slot_size * OUT) + 1e-06)
    merged_out = (
        (blocks / req_norm[:, None, None]).astype(jnp.bfloat16).reshape(IMG_ROW * most, out_dev)
    )
    return (merged_out, req_norm, peaks)


def solution(mesh):
    in_specs = (
        P(("row", "col"), None),
        P(),
        P(),
        P(),
        P(),
        P(None, "row", "col"),
        P(None, "col", "row"),
        P(None, "row", "col"),
        P(None, "col", "row"),
        P(),
        P(),
        P("row", "col"),
    )
    out_specs = (P("row", "col"), P("row"), P("row"))
    return jax.shard_map(local, mesh=mesh, in_specs=in_specs, out_specs=out_specs, check_vma=False)
```

profile of v0, /device:TPU:1, one launch (start us, length us, event | category | flops | bytes accessed | tf_op | source)
XLA Modules:
  0.0 487.1 jit_solution(6885048592995645499)
XLA Ops:
  7.2 0.7 all-gather.23.cloned.1.call-update
  7.9 0.8 slice_reduce_fusion
  8.8 1.1 convert_reduce_fusion.1
  9.9 1.2 fusion.45
  11.1 2.0 fusion.48
  13.2 0.9 dynamic-slice_reduce_fusion
  14.0 0.2 reduce-window.8
  14.2 0.9 copy.48
  15.1 22.5 %all-gather.1 = bf16[1,160,1280]{1,0,2:T(2,128)(2,1)S(1)} all-gather(bf16[1,160,80]{1,0,2:T(2,128)(2,1)S(1)} %copy.48), channel_id=3, replica_groups=mesh['row'=16,'col'=8] {'row'}, dimensions={2}, use_global_device_ids=true | all-gather | bytes 435200 | tf_op jit(solution)/shard_map/all_gather | solution.py:83
  37.6 1.8 copy.49
  39.5 0.7 broadcast_compare_fusion.1
  40.2 14.8 %all-gather.23.cloned.1.call-done = bf16[1,1280,480]{2,1,0:T(8,128)(2,1)} async-done(((bf16[1,80,480]{2,1,0:T(8,128)(2,1)}), bf16[1,1280,480]{2,1,0:T(8,128)(2,1)}) %all-gather.23.cloned.1.call-update) | async-done | bytes 1228816 | tf_op jit(solution)/shard_map/all_gather | solution.py:76
  55.0 30.0 %all-gather.13.cloned.1.call-done = bf16[1024,1280]{1,0:T(8,128)(2,1)} async-done(((bf16[128,1280]{1,0:T(8,128)(2,1)}), bf16[1024,1280]{1,0:T(8,128)(2,1)}) %all-gather.13.cloned.1.call-update) | async-done | bytes 2621456 | tf_op jit(solution)/shard_map/all_gather | solution.py:72
  85.1 3.6 convolution_convert_fusion.2
  88.6 3.7 fusion.112
  92.3 3.6 fusion.111
  95.9 3.2 fusion.31
  99.1 0.3 copy-done.6
  99.4 0.8 fusion.30
  100.2 2.4 convolution_convert_fusion.1
  102.7 0.5 all-gather.25.cloned.1.call-update
  103.3 0.5 all-gather.27.cloned.1.call-update
  103.9 31.0 %reduce-scatter.3.cloned.1.call-done = bf16[128,1280]{1,0:T(8,128)(2,1)} async-done(((bf16[1024,1280]{1,0:T(8,128)(2,1)}), bf16[128,1280]{1,0:T(8,128)(2,1)}) %reduce-scatter.3.cloned.1.call-update) | async-done | bytes 327696 | tf_op jit(solution)/shard_map/reduce_scatter | solution.py:86
  134.9 1.1 convert_reduce_fusion
  136.0 0.2 fusion.41
  136.3 1.0 fusion.44
  137.3 0.2 reduce-scatter.5.cloned.1.call-start
  137.5 43.5 %all-gather.25.cloned.1.call-done = bf16[1,1280,640]{2,1,0:T(8,128)(2,1)} async-done(((bf16[1,80,640]{2,1,0:T(8,128)(2,1)}), bf16[1,1280,640]{2,1,0:T(8,128)(2,1)}) %all-gather.25.cloned.1.call-update) | async-done | bytes 1638416 | tf_op jit(solution)/shard_map/all_gather | solution.py:97
  181.0 45.1 %all-gather.27.cloned.1.call-done = bf16[1,640,1280]{1,2,0:T(8,128)(2,1)} async-done(((bf16[1,640,80]{1,2,0:T(8,128)(2,1)}), bf16[1,640,1280]{1,2,0:T(8,128)(2,1)}) %all-gather.27.cloned.1.call-update) | async-done | bytes 1638416 | tf_op jit(solution)/shard_map/all_gather | solution.py:103
  226.1 29.3 %all-gather.15.cloned.1.call-done = bf16[1024,1280]{1,0:T(8,128)(2,1)} async-done(((bf16[128,1280]{1,0:T(8,128)(2,1)}), bf16[1024,1280]{1,0:T(8,128)(2,1)}) %all-gather.15.cloned.1.call-update) | async-done | bytes 2621456 | tf_op jit(solution)/shard_map/all_gather | solution.py:93
  255.3 13.0 %convolution_convert_fusion = bf16[1024,1280]{1,0:T(8,128)(2,1)} fusion(bf16[1,640,1280]{1,2,0:T(8,128)(2,1)} %all-gather.27.cloned.1.call-done, bf16[1024,1280]{1,0:T(8,128)(2,1)} %all-gather.15.cloned.1.call-done, bf16[1,1280,640]{2,1,0:T(8,128)(2,1)} %all-gather.25.cloned.1.call-done), kind=kOutput, calls=%fused_computation.12 | convolution fusion | flops 3399352320 | bytes 8519680 | tf_op jit(solution)/shard_map/dot_general | solution.py:101
  268.4 0.7 all-gather.19.cloned.1.call-update
  269.2 31.4 %reduce-scatter.5.cloned.1.call-done = bf16[128,1280]{1,0:T(8,128)(2,1)} async-done(((bf16[1024,1280]{1,0:T(8,128)(2,1)}), bf16[128,1280]{1,0:T(8,128)(2,1)}) %reduce-scatter.5.cloned.1.call-update) | async-done | bytes 327696 | tf_op jit(solution)/shard_map/reduce_scatter | solution.py:106
  300.6 1.1 convert_reduce_fusion.2
  301.7 1.2 fusion.49
  302.9 1.2 fusion.52
  304.1 0.9 reshape.280
  305.1 55.3 %all-gather.19.cloned.1.call-done = bf16[5120,512]{1,0:T(8,128)(2,1)} async-done(((bf16[320,512]{1,0:T(8,128)(2,1)}), bf16[5120,512]{1,0:T(8,128)(2,1)}) %all-gather.19.cloned.1.call-update) | async-done | bytes 5242896 | tf_op jit(solution)/shard_map/all_gather | solution.py:117
  360.4 28.6 %all-gather.17.cloned.1.call-done = bf16[256,5120]{1,0:T(8,128)(2,1)} async-done(((bf16[32,5120]{1,0:T(8,128)(2,1)}), bf16[256,5120]{1,0:T(8,128)(2,1)}) %all-gather.17.cloned.1.call-update) | async-done | bytes 2621456 | tf_op jit(solution)/shard_map/all_gather | solution.py:112
  389.0 5.5 %convolution_convert_fusion.3 = bf16[256,512]{1,0:T(8,128)(2,1)} fusion(bf16[256,5120]{1,0:T(8,128)(2,1)} %all-gather.17.cloned.1.call-done, bf16[5120,512]{1,0:T(8,128)(2,1)} %all-gather.19.cloned.1.call-done), kind=kOutput, calls=%fused_computation.47 | convolution fusion | flops 1342308352 | bytes 8126464 | tf_op jit(solution)/shard_map/dot_general | solution.py:115
  395.0 0.6 gather_fusion.1
  396.1 0.6 gather_fusion
  397.0 48.9 %all-gather.21.cloned.1.call-done = bf16[4096,512]{1,0:T(8,128)(2,1)} async-done(((bf16[256,512]{1,0:T(8,128)(2,1)}), bf16[4096,512]{1,0:T(8,128)(2,1)}) %all-gather.21.cloned.1.call-update) | async-done | bytes 4194320 | tf_op jit(solution)/shard_map/all_gather | solution.py:134
  445.8 4.8 gather_fusion.2
  450.6 0.4 fusion.34
  451.2 12.7 %psum.7 = f32[8]{0:T(128)S(1)} all-reduce(f32[8]{0:T(128)S(1)} %reduce_sum.118), channel_id=1, replica_groups=mesh['row'=16,'col'=8] {'col'}, use_global_device_ids=true, to_apply=%region_18.19 | all-reduce | flops 8 | bytes 64 | tf_op jit(solution)/shard_map/psum | solution.py:141
  464.3 15.0 %pmax.7 = f32[8]{0:T(128)} all-reduce(f32[8]{0:T(128)S(1)} %reduce_max.38), channel_id=1, replica_groups=mesh['row'=16,'col'=8] {'col'}, use_global_device_ids=true, to_apply=%region_21.22 | all-reduce | flops 8 | bytes 64 | tf_op jit(solution)/shard_map/pmax | solution.py:142
  479.3 0.9 fusion.33
  (62 shorter events, 2.3 us)
Async XLA Ops:
  7.2 47.9 %all-gather.23.cloned.1.call-start = ((), (), s32[]{:S(2)}) async-start(), calls=%async_computation.9 | async-start | bytes 1392640 | tf_op jit(solution)/shard_map/all_gather | solution.py:76
  7.9 77.2 %all-gather.13.cloned.1.call-start = ((), (), s32[]{:S(2)}) async-start(), calls=%async_computation.2 | async-start | bytes 2949120 | tf_op jit(solution)/shard_map/all_gather | solution.py:72
  13.1 121.8 %reduce-scatter.3.cloned.1.call-start = ((), (), s32[]{:S(2)}) async-start(), calls=%async_computation.3 | async-start | bytes 2949120 | tf_op jit(solution)/shard_map/reduce_scatter | solution.py:86
  95.9 3.4 copy-start.6
  100.2 34.7 %copy-start = (bf16[128,1280]{1,0:T(8,128)(2,1)S(1)}, bf16[128,1280]{1,0:T(8,128)(2,1)}, u32[]{:S(2)}) copy-start(bf16[128,1280]{1,0:T(8,128)(2,1)} %param.12) | copy-start | bytes 983044
  102.7 78.3 %all-gather.25.cloned.1.call-start = ((), (), s32[]{:S(2)}) async-start(), calls=%async_computation.10 | async-start | bytes 1740800 | tf_op jit(solution)/shard_map/all_gather | solution.py:97
  103.3 122.8 %all-gather.27.cloned.1.call-start = ((), (), s32[]{:S(2)}) async-start(), calls=%async_computation.11 | async-start | bytes 1740800 | tf_op jit(solution)/shard_map/all_gather | solution.py:103
  103.8 151.5 %all-gather.15.cloned.1.call-start = ((), (), s32[]{:S(2)}) async-start(), calls=%async_computation.4 | async-start | bytes 2949120 | tf_op jit(solution)/shard_map/all_gather | solution.py:93
  137.3 163.3 %reduce-scatter.5.cloned.1.call-start = ((), (), s32[]{:S(2)}) async-start(), calls=%async_computation.5 | async-start | bytes 2949120 | tf_op jit(solution)/shard_map/reduce_scatter | solution.py:106
  268.3 34.6 %copy-start.2 = (f32[1280]{0:T(1024)S(1)}, f32[1280]{0:T(1024)}, u32[]{:S(2)}) copy-start(f32[1280]{0:T(1024)} %param.22) | copy-start | bytes 15364
  268.3 34.6 %copy-start.3 = (f32[1280]{0:T(1024)S(1)}, f32[1280]{0:T(1024)}, u32[]{:S(2)}) copy-start(f32[1280]{0:T(1024)} %param.21) | copy-start | bytes 15364
  268.4 92.0 %all-gather.19.cloned.1.call-start = ((), (), s32[]{:S(2)}) async-start(), calls=%async_computation.7 | async-start | bytes 5570560 | tf_op jit(solution)/shard_map/all_gather | solution.py:117
  269.1 119.9 %all-gather.17.cloned.1.call-start = ((), (), s32[]{:S(2)}) async-start(), calls=%async_computation.6 | async-start | bytes 2949120 | tf_op jit(solution)/shard_map/all_gather | solution.py:112
  305.1 89.5 %copy-start.1 = (s32[16,8]{0,1:T(8,128)S(1)}, s32[16,8]{0,1:T(8,128)}, u32[]{:S(2)}) copy-start(s32[16,8]{0,1:T(8,128)} %param.13) | copy-start | bytes 1540
  305.1 89.7 %copy-start.5 = (s32[128]{0:T(128)S(1)}, s32[128]{0:T(128)}, u32[]{:S(2)}) copy-start(s32[128]{0:T(128)} %param.14) | copy-start | bytes 1540
  305.1 140.7 %all-gather.21.cloned.1.call-start = ((), (), s32[]{:S(2)}) async-start(), calls=%async_computation.8 | async-start | bytes 4456448 | tf_op jit(solution)/shard_map/all_gather | solution.py:134
  464.0 16.3 %copy-start.4 = (f32[8]{0:T(128)}, f32[8]{0:T(128)S(1)}, u32[]{:S(2)}) copy-start(f32[8]{0:T(128)S(1)} %add_sqrt_fusion) | copy-start | bytes 100
Sparse Core Ops, SparseCore 0:
  10.1 44.8 all-gather.22
  57.3 27.7 all-gather.12
  102.8 32.0 reduce-scatter.2
  136.9 44.0 all-gather.24
  183.0 43.0 all-gather.26
  228.2 27.1 all-gather.14
  268.5 32.0 reduce-scatter.4
  302.7 57.6 all-gather.18
  362.7 26.2 all-gather.16
  394.7 51.1 all-gather.20
where the time goes:
time: 488 us; the launch traced here: 487 us
  waiting for transfers between devices  360 us (74%)
  blocking collectives  50.3 us (10%)
  matrix products  35.8 us (7%)
  between operations  14.4 us (3%)
  other arithmetic  13.2 us (3%)
  local copies, waits for them, and re-layouts  12.6 us (3%)
    all_gather x1, waiting for transfers between devices, local(): lax.all_gather(w_merge, 'row', axis=0, tiled=True)  55.3 us
    all_gather x1, waiting for transfers between devices, local(): piece = lax.all_gather(projected, 'row', axis=0, tiled=True)  48.9 us
    all_gather x1, waiting for transfers between devices, local(): lax.all_gather(w_down[0], 'row', axis=1, tiled=True)  45.1 us
    all_gather x1, waiting for transfers between devices, local(): lax.all_gather(w_up[0], 'row', axis=0, tiled=True)  43.5 us
    reduce_scatter x1, waiting for transfers between devices, local(): lax.psum_scatter(mlp_terms.astype(jnp.bfloat16), 'col', scatter_dimension...  31.4 us
    reduce_scatter x1, waiting for transfers between devices, local(): lax.psum_scatter(attn_terms.astype(jnp.bfloat16), 'col', scatter_dimensio...  31 us
    all_gather x1, waiting for transfers between devices, local(): normed_all = lax.all_gather(normed, 'col', axis=0, tiled=True)  30 us
    all_gather x1, waiting for transfers between devices, local(): normed_mlp = lax.all_gather(normed, 'col', axis=0, tiled=True)  29.3 us
  transfers between devices with their start and end apart: 10, of which 10 were waited for; matrix products, arithmetic and copies ran while one was open for 4% of the time, Pallas kernels for 0%

commit v1 on v0

--- a/solution.py
+++ b/solution.py
@@ -69,7 +69,43 @@
     normed = layer_norm(stream.astype(jnp.float32), ln_gain[0, 0], ln_bias[0, 0]).astype(
         jnp.bfloat16
     )
-    normed_all = lax.all_gather(normed, "col", axis=0, tiled=True)
+
+    def prepare_view(t0):
+        opened = lax.axis_size("col")
+        carry = lax.axis_index("col")
+        g_now, small, fresh = (opened, carry, t0.shape[0])
+        step_out = lax.dynamic_update_slice_in_dim(
+            jnp.zeros(
+                [s * g_now if dev_j == 0 else s for dev_j, s in enumerate(t0.shape)], t0.dtype
+            ),
+            t0,
+            small * fresh,
+            axis=0,
+        )
+        finding = top = t0
+        k0 = 1
+        while k0 < g_now // 2 + 1:
+            finding = lax.ppermute(
+                finding,
+                axis_name="col",
+                perm=[(dev_j, (dev_j + 1) % g_now) for dev_j in range(g_now)],
+            )
+            step_out = lax.dynamic_update_slice_in_dim(
+                step_out, finding, (small - k0) % g_now * fresh, axis=0
+            )
+            if 2 * k0 < g_now:
+                top = lax.ppermute(
+                    top,
+                    axis_name="col",
+                    perm=[(dev_j, (dev_j - 1) % g_now) for dev_j in range(g_now)],
+                )
+                step_out = lax.dynamic_update_slice_in_dim(
+                    step_out, top, (small + k0) % g_now * fresh, axis=0
+                )
+            k0 = k0 + 1
+        return step_out
+
+    normed_all = prepare_view(normed)
     left_part = normed_all
     qkv = jnp.dot(
         left_part,

time: 488 us -> 470 us (0.963)
  waiting for transfers between devices: 360 us -> 324 us
  starting transfers between devices: 0.58 us -> 16.2 us
  local copies, waits for them, and re-layouts: 12.6 us -> 18.1 us
    all_gather x1 -> x0, waiting for transfers between devices: 30 us -> none  [local(): normed_all = lax.all_gather(normed, 'col', axis=0, tiled=True)]
    ppermute x0 -> x7, starting transfers between devices: none -> 15.7 us  [the longest x4 15 us: prepare_view(): lax.ppermute(finding, axis_name='col', perm=[(dev_j, (dev_j + 1) % g_now)...]
    all_gather x1, waiting for transfers between devices: 14.8 us -> 0.01 us  [local(): lax.all_gather(w_qkv[0], 'row', axis=0, tiled=True)]
    ppermute x0 -> x7, waiting for transfers between devices: none -> 6.87 us  [the longest x4 6.46 us: prepare_view(): lax.ppermute(finding, axis_name='col', perm=[(dev_j, (dev_j + 1) % g_now)...]
    dynamic_update_slice x0 -> x7, local copies, waits for them, and re-layouts: none -> 5.24 us  [the longest x4 2.96 us: prepare_view(): lax.dynamic_update_slice_in_dim(step_out, finding, (small - k0) % g_now *...]
  transfers between devices with their start and end apart: 10 -> 16, of which waited for: 10 -> 12; matrix products, arithmetic and copies ran while one was open for 4% -> 4% of each run, Pallas kernels for 0% -> 0%
where the time goes in v1:
time: 470 us
  waiting for transfers between devices  324 us (69%)
  blocking collectives  49.1 us (10%)
  matrix products  35.8 us (8%)
  local copies, waits for them, and re-layouts  18.1 us (4%)
  starting transfers between devices  16.2 us (3%)
  between operations  14.2 us (3%)
  other arithmetic  12.3 us (3%)
    all_gather x1, waiting for transfers between devices, local(): lax.all_gather(w_merge, 'row', axis=0, tiled=True)  55.3 us
    all_gather x1, waiting for transfers between devices, local(): piece = lax.all_gather(projected, 'row', axis=0, tiled=True)  48.9 us
    all_gather x1, waiting for transfers between devices, local(): lax.all_gather(w_down[0], 'row', axis=1, tiled=True)  45.1 us
    all_gather x1, waiting for transfers between devices, local(): lax.all_gather(w_up[0], 'row', axis=0, tiled=True)  43.6 us
    reduce_scatter x1, waiting for transfers between devices, local(): lax.psum_scatter(attn_terms.astype(jnp.bfloat16), 'col', scatter_dimensio...  32.9 us
    reduce_scatter x1, waiting for transfers between devices, local(): lax.psum_scatter(mlp_terms.astype(jnp.bfloat16), 'col', scatter_dimension...  31.4 us
    all_gather x1, waiting for transfers between devices, local(): normed_mlp = lax.all_gather(normed, 'col', axis=0, tiled=True)  29.3 us
    all_gather x1, waiting for transfers between devices, local(): merged_all = lax.all_gather(merged, 'col', axis=0, tiled=True)  28.6 us
  transfers between devices with their start and end apart: 16, of which 12 were waited for; matrix products, arithmetic and copies ran while one was open for 4% of the time, Pallas kernels for 0%

profile of v1, /device:TPU:1, one launch (start us, length us, event | category | flops | bytes accessed | tf_op | source)
XLA Modules:
  0.0 469.5 jit_solution(10143123524472847171)
XLA Ops:
  7.2 1.1 convert_reduce_fusion.1
  8.4 1.2 fusion.45
  9.6 0.8 slice_reduce_fusion
  10.5 1.7 broadcast_in_dim.56
  12.2 1.0 constant_dynamic-update-slice_fusion.7
  13.1 3.0 collective-permute-start
  16.9 21.3 %all-gather.1 = bf16[1,160,1280]{1,0,2:T(2,128)(2,1)S(1)} all-gather(bf16[1,160,80]{1,0,2:T(2,128)(2,1)S(1)} %copy.48), channel_id=3, replica_groups=mesh['row'=16,'col'=8] {'row'}, dimensions={2}, use_global_device_ids=true | all-gather | bytes 435200 | tf_op jit(solution)/shard_map/all_gather | solution.py:119
  38.3 1.8 copy.49
  40.9 7.0 %collective-permute-start.2 = (bf16[128,1280]{1,0:T(8,128)(2,1)S(1)}, bf16[128,1280]{1,0:T(8,128)(2,1)S(1)}, u32[]{:S(2)}, u32[]{:S(2)}) collective-permute-start(bf16[128,1280]{1,0:T(8,128)(2,1)S(1)} %collective-permute-done), channel_id=1, source_target_pairs={{0,1},{1,2},{2,3},{3,4},{4,5},{5,6},{6,7},{7,0},{8,9},{9,10},{10,1... | collective-permute-start | bytes 983048 | tf_op jit(solution)/shard_map/ppermute | solution.py:88
  47.9 0.7 constant_dynamic-update-slice_fusion.6
  48.6 0.7 constant_dynamic-update-slice_fusion.5
  49.4 2.5 collective-permute-done.2
  51.9 2.5 collective-permute-start.4
  55.5 0.7 constant_dynamic-update-slice_fusion.4
  56.2 0.8 constant_dynamic-update-slice_fusion.3
  57.0 1.4 collective-permute-done.4
  58.4 2.5 collective-permute-start.6
  60.9 0.8 constant_dynamic-update-slice_fusion.2
  61.6 0.8 constant_dynamic-update-slice_fusion.1
  62.4 2.5 collective-permute-done.6
  64.9 0.7 constant_dynamic-update-slice_fusion
  65.6 3.6 convolution_convert_fusion.2
  69.2 3.7 fusion.113
  72.9 3.6 fusion.112
  76.5 3.2 fusion.31
  80.0 0.9 fusion.30
  80.8 2.4 convolution_convert_fusion.1
  84.6 32.9 %reduce-scatter.3.cloned.1.call-done = bf16[128,1280]{1,0:T(8,128)(2,1)} async-done(((bf16[1024,1280]{1,0:T(8,128)(2,1)}), bf16[128,1280]{1,0:T(8,128)(2,1)}) %reduce-scatter.3.cloned.1.call-update) | async-done | bytes 327696 | tf_op jit(solution)/shard_map/reduce_scatter | solution.py:122
  117.5 1.2 convert_reduce_fusion
  118.9 1.0 fusion.44
  120.2 43.6 %all-gather.22.cloned.1.call-done = bf16[1,1280,640]{2,1,0:T(8,128)(2,1)} async-done(((bf16[1,80,640]{2,1,0:T(8,128)(2,1)}), bf16[1,1280,640]{2,1,0:T(8,128)(2,1)}) %all-gather.22.cloned.1.call-update) | async-done | bytes 1638416 | tf_op jit(solution)/shard_map/all_gather | solution.py:133
  163.8 45.1 %all-gather.24.cloned.1.call-done = bf16[1,640,1280]{1,2,0:T(8,128)(2,1)} async-done(((bf16[1,640,80]{1,2,0:T(8,128)(2,1)}), bf16[1,640,1280]{1,2,0:T(8,128)(2,1)}) %all-gather.24.cloned.1.call-update) | async-done | bytes 1638416 | tf_op jit(solution)/shard_map/all_gather | solution.py:139
  208.8 29.3 %all-gather.12.cloned.1.call-done = bf16[1024,1280]{1,0:T(8,128)(2,1)} async-done(((bf16[128,1280]{1,0:T(8,128)(2,1)}), bf16[1024,1280]{1,0:T(8,128)(2,1)}) %all-gather.12.cloned.1.call-update) | async-done | bytes 2621456 | tf_op jit(solution)/shard_map/all_gather | solution.py:129
  238.1 13.0 %convolution_convert_fusion = bf16[1024,1280]{1,0:T(8,128)(2,1)} fusion(bf16[1,640,1280]{1,2,0:T(8,128)(2,1)} %all-gather.24.cloned.1.call-done, bf16[1024,1280]{1,0:T(8,128)(2,1)} %all-gather.12.cloned.1.call-done, bf16[1,1280,640]{2,1,0:T(8,128)(2,1)} %all-gather.22.cloned.1.call-done), kind=kOutput, calls=%fused_computation.12 | convolution fusion | flops 3399352320 | bytes 8519680 | tf_op jit(solution)/shard_map/dot_general | solution.py:137
  251.2 0.7 all-gather.16.cloned.1.call-update
  251.9 31.4 %reduce-scatter.5.cloned.1.call-done = bf16[128,1280]{1,0:T(8,128)(2,1)} async-done(((bf16[1024,1280]{1,0:T(8,128)(2,1)}), bf16[128,1280]{1,0:T(8,128)(2,1)}) %reduce-scatter.5.cloned.1.call-update) | async-done | bytes 327696 | tf_op jit(solution)/shard_map/reduce_scatter | solution.py:142
  283.3 1.1 convert_reduce_fusion.2
  284.5 1.2 fusion.49
  285.7 1.2 fusion.52
  286.9 0.9 reshape.280
  287.9 55.3 %all-gather.16.cloned.1.call-done = bf16[5120,512]{1,0:T(8,128)(2,1)} async-done(((bf16[320,512]{1,0:T(8,128)(2,1)}), bf16[5120,512]{1,0:T(8,128)(2,1)}) %all-gather.16.cloned.1.call-update) | async-done | bytes 5242896 | tf_op jit(solution)/shard_map/all_gather | solution.py:153
  343.2 28.6 %all-gather.14.cloned.1.call-done = bf16[256,5120]{1,0:T(8,128)(2,1)} async-done(((bf16[32,5120]{1,0:T(8,128)(2,1)}), bf16[256,5120]{1,0:T(8,128)(2,1)}) %all-gather.14.cloned.1.call-update) | async-done | bytes 2621456 | tf_op jit(solution)/shard_map/all_gather | solution.py:148
  371.8 5.5 %convolution_convert_fusion.3 = bf16[256,512]{1,0:T(8,128)(2,1)} fusion(bf16[256,5120]{1,0:T(8,128)(2,1)} %all-gather.14.cloned.1.call-done, bf16[5120,512]{1,0:T(8,128)(2,1)} %all-gather.16.cloned.1.call-done), kind=kOutput, calls=%fused_computation.47 | convolution fusion | flops 1342308352 | bytes 8126464 | tf_op jit(solution)/shard_map/dot_general | solution.py:151
  379.7 48.9 %all-gather.18.cloned.1.call-done = bf16[4096,512]{1,0:T(8,128)(2,1)} async-done(((bf16[256,512]{1,0:T(8,128)(2,1)}), bf16[4096,512]{1,0:T(8,128)(2,1)}) %all-gather.18.cloned.1.call-update) | async-done | bytes 4194320 | tf_op jit(solution)/shard_map/all_gather | solution.py:170
  428.6 4.8 %gather_fusion.2 = bf16[384,512]{1,0:T(8,128)(2,1)S(1)} fusion(bf16[4096,512]{1,0:T(8,128)(2,1)} %all-gather.18.cloned.1.call-done, s32[1024]{0:T(1024)S(1)} %pad_clamp_fusion), kind=kCustom, calls=%fused_computation.2 | custom fusion | bytes 787968 | tf_op jit(solution)/shard_map/jit(_take)/gather | solution.py:172
  434.0 12.7 %psum.7 = f32[8]{0:T(128)S(1)} all-reduce(f32[8]{0:T(128)S(1)} %reduce_sum.118), channel_id=1, replica_groups=mesh['row'=16,'col'=8] {'col'}, use_global_device_ids=true, to_apply=%region_18.19 | all-reduce | flops 8 | bytes 64 | tf_op jit(solution)/shard_map/psum | solution.py:177
  447.1 15.0 %pmax.7 = f32[8]{0:T(128)} all-reduce(f32[8]{0:T(128)S(1)} %reduce_max.38), channel_id=1, replica_groups=mesh['row'=16,'col'=8] {'col'}, use_global_device_ids=true, to_apply=%region_21.22 | all-reduce | flops 8 | bytes 64 | tf_op jit(solution)/shard_map/pmax | solution.py:178
  462.1 0.9 fusion.33
  (83 shorter events, 8.1 us)
Async XLA Ops:
  7.2 5.0 %copy-start = (bf16[128,1280]{1,0:T(8,128)(2,1)S(1)}, bf16[128,1280]{1,0:T(8,128)(2,1)}, u32[]{:S(2)}) copy-start(bf16[128,1280]{1,0:T(8,128)(2,1)} %param.12) | copy-start | bytes 983044
  7.2 9.1 %copy-start.1 = (s32[16,8]{0,1:T(8,128)S(1)}, s32[16,8]{0,1:T(8,128)}, u32[]{:S(2)}) copy-start(s32[16,8]{0,1:T(8,128)} %param.13) | copy-start | bytes 1540
  7.2 9.5 %copy-start.2 = (bf16[1,160,80]{2,1,0:T(8,128)(2,1)S(1)}, bf16[1,160,80]{2,1,0:T(8,128)(2,1)}, u32[]{:S(2)}) copy-start(bf16[1,160,80]{2,1,0:T(8,128)(2,1)} %param.18) | copy-start | bytes 76804
  7.2 58.4 %all-gather.20.cloned.1.call-start = ((), (), s32[]{:S(2)}) async-start(), calls=%async_computation.8 | async-start | bytes 1392640 | tf_op jit(solution)/shard_map/all_gather | solution.py:112
  13.1 27.7 %collective-permute-start = (bf16[128,1280]{1,0:T(8,128)(2,1)S(1)}, bf16[128,1280]{1,0:T(8,128)(2,1)S(1)}, u32[]{:S(2)}, u32[]{:S(2)}) collective-permute-start(bf16[128,1280]{1,0:T(8,128)(2,1)S(1)} %get-tuple-element.13), channel_id=1, source_target_pairs={{0,1},{1,2},{2,3},{3,4},{4,5},{5,6},{6,7},{7,0},{8,9},{9,10},{10,1... | collective-permute-start | bytes 983048 | tf_op jit(solution)/shard_map/ppermute | solution.py:88
  16.2 31.7 %collective-permute-start.1 = (bf16[128,1280]{1,0:T(8,128)(2,1)S(1)}, bf16[128,1280]{1,0:T(8,128)(2,1)S(1)}, u32[]{:S(2)}, u32[]{:S(2)}) collective-permute-start(bf16[128,1280]{1,0:T(8,128)(2,1)S(1)} %get-tuple-element.13), channel_id=1, source_target_pairs={{0,7},{1,0},{2,1},{3,2},{4,3},{5,4},{6,5},{7,6},{8,15},{9,8},{10,9... | collective-permute-start | bytes 983048 | tf_op jit(solution)/shard_map/ppermute | solution.py:97
  16.2 101.3 %reduce-scatter.3.cloned.1.call-start = ((), (), s32[]{:S(2)}) async-start(), calls=%async_computation.2 | async-start | bytes 2949120 | tf_op jit(solution)/shard_map/reduce_scatter | solution.py:122
  40.9 11.0 %collective-permute-start.2 = (bf16[128,1280]{1,0:T(8,128)(2,1)S(1)}, bf16[128,1280]{1,0:T(8,128)(2,1)S(1)}, u32[]{:S(2)}, u32[]{:S(2)}) collective-permute-start(bf16[128,1280]{1,0:T(8,128)(2,1)S(1)} %collective-permute-done), channel_id=1, source_target_pairs={{0,1},{1,2},{2,3},{3,4},{4,5},{5,6},{6,7},{7,0},{8,9},{9,10},{10,1... | collective-permute-start | bytes 983048 | tf_op jit(solution)/shard_map/ppermute | solution.py:88
  47.9 6.9 %collective-permute-start.3 = (bf16[128,1280]{1,0:T(8,128)(2,1)S(1)}, bf16[128,1280]{1,0:T(8,128)(2,1)S(1)}, u32[]{:S(2)}, u32[]{:S(2)}) collective-permute-start(bf16[128,1280]{1,0:T(8,128)(2,1)S(1)} %collective-permute-done.1), channel_id=1, source_target_pairs={{0,7},{1,0},{2,1},{3,2},{4,3},{5,4},{6,5},{7,6},{8,15},{9,8},{10,9... | collective-permute-start | bytes 983048 | tf_op jit(solution)/shard_map/ppermute | solution.py:97
  51.9 6.5 %collective-permute-start.4 = (bf16[128,1280]{1,0:T(8,128)(2,1)S(1)}, bf16[128,1280]{1,0:T(8,128)(2,1)S(1)}, u32[]{:S(2)}, u32[]{:S(2)}) collective-permute-start(bf16[128,1280]{1,0:T(8,128)(2,1)S(1)} %collective-permute-done.2), channel_id=1, source_target_pairs={{0,1},{1,2},{2,3},{3,4},{4,5},{5,6},{6,7},{7,0},{8,9},{9,10},{10,1... | collective-permute-start | bytes 983048 | tf_op jit(solution)/shard_map/ppermute | solution.py:88
  54.8 6.9 %collective-permute-start.5 = (bf16[128,1280]{1,0:T(8,128)(2,1)S(1)}, bf16[128,1280]{1,0:T(8,128)(2,1)S(1)}, u32[]{:S(2)}, u32[]{:S(2)}) collective-permute-start(bf16[128,1280]{1,0:T(8,128)(2,1)S(1)} %collective-permute-done.3), channel_id=1, source_target_pairs={{0,7},{1,0},{2,1},{3,2},{4,3},{5,4},{6,5},{7,6},{8,15},{9,8},{10,9... | collective-permute-start | bytes 983048 | tf_op jit(solution)/shard_map/ppermute | solution.py:97
  58.4 6.5 %collective-permute-start.6 = (bf16[128,1280]{1,0:T(8,128)(2,1)S(1)}, bf16[128,1280]{1,0:T(8,128)(2,1)S(1)}, u32[]{:S(2)}, u32[]{:S(2)}) collective-permute-start(bf16[128,1280]{1,0:T(8,128)(2,1)S(1)} %collective-permute-done.4), channel_id=1, source_target_pairs={{0,1},{1,2},{2,3},{3,4},{4,5},{5,6},{6,7},{7,0},{8,9},{9,10},{10,1... | collective-permute-start | bytes 983048 | tf_op jit(solution)/shard_map/ppermute | solution.py:88
  76.5 3.4 copy-start.7
  83.3 80.5 %all-gather.22.cloned.1.call-start = ((), (), s32[]{:S(2)}) async-start(), calls=%async_computation.9 | async-start | bytes 1740800 | tf_op jit(solution)/shard_map/all_gather | solution.py:133
  84.0 124.8 %all-gather.24.cloned.1.call-start = ((), (), s32[]{:S(2)}) async-start(), calls=%async_computation.10 | async-start | bytes 1740800 | tf_op jit(solution)/shard_map/all_gather | solution.py:139
  84.6 153.5 %all-gather.12.cloned.1.call-start = ((), (), s32[]{:S(2)}) async-start(), calls=%async_computation.3 | async-start | bytes 2949120 | tf_op jit(solution)/shard_map/all_gather | solution.py:129
  119.9 163.4 %reduce-scatter.5.cloned.1.call-start = ((), (), s32[]{:S(2)}) async-start(), calls=%async_computation.4 | async-start | bytes 2949120 | tf_op jit(solution)/shard_map/reduce_scatter | solution.py:142
  251.1 34.5 %copy-start.3 = (f32[1280]{0:T(1024)S(1)}, f32[1280]{0:T(1024)}, u32[]{:S(2)}) copy-start(f32[1280]{0:T(1024)} %param.22) | copy-start | bytes 15364
  251.1 34.5 %copy-start.4 = (f32[1280]{0:T(1024)S(1)}, f32[1280]{0:T(1024)}, u32[]{:S(2)}) copy-start(f32[1280]{0:T(1024)} %param.21) | copy-start | bytes 15364
  251.1 92.0 %all-gather.16.cloned.1.call-start = ((), (), s32[]{:S(2)}) async-start(), calls=%async_computation.6 | async-start | bytes 5570560 | tf_op jit(solution)/shard_map/all_gather | solution.py:153
  251.9 119.9 %all-gather.14.cloned.1.call-start = ((), (), s32[]{:S(2)}) async-start(), calls=%async_computation.5 | async-start | bytes 2949120 | tf_op jit(solution)/shard_map/all_gather | solution.py:148
  287.8 89.8 %copy-start.6 = (s32[128]{0:T(128)S(1)}, s32[128]{0:T(128)}, u32[]{:S(2)}) copy-start(s32[128]{0:T(128)} %param.14) | copy-start | bytes 1540
  287.8 140.8 %all-gather.18.cloned.1.call-start = ((), (), s32[]{:S(2)}) async-start(), calls=%async_computation.7 | async-start | bytes 4456448 | tf_op jit(solution)/shard_map/all_gather | solution.py:170
  446.7 16.3 %copy-start.5 = (f32[8]{0:T(128)}, f32[8]{0:T(128)S(1)}, u32[]{:S(2)}) copy-start(f32[8]{0:T(128)S(1)} %add_sqrt_fusion) | copy-start | bytes 100
Sparse Core Ops, SparseCore 0:
  16.3 43.4 all-gather.19
  83.4 34.0 reduce-scatter.2
  119.6 44.0 all-gather.21
  165.8 43.0 all-gather.23
  211.0 27.1 all-gather.11
  251.3 31.9 reduce-scatter.4
  285.4 57.6 all-gather.15
  345.4 26.2 all-gather.13
  377.4 51.1 all-gather.17
